TPU v7x, 512 devices: a whole 4x4x16 slice. The times are simulated.
512 devices in a mesh: nodes: 64 (over x, z), heads: 8 (over y, core).
Axes of the slice: x: 4, y: 4, z: 16, core: 2. Of those that a mesh axis runs over, the one named last changes fastest.
Arguments:
- hidden: bfloat16 [64, 7168], P('nodes'), may hold values from -6 to 6
- norm_gain: float32 [7168], replicated, may hold values from 0.1 to 1.9
- qkv_weight: bfloat16 [7168, 56, 384], P('nodes', 'heads'), may hold values from -0.0625 to 0.0625
- out_weight: bfloat16 [7168, 7168], P('heads', 'nodes'), may hold values from -0.0625 to 0.0625
- prefix_keys: bfloat16 [256, 128, 56, 128], P('nodes', None, 'heads'), may hold values from -1000 to 1000
- prefix_values: bfloat16 [256, 128, 56, 128], P('nodes', None, 'heads'), may hold values from -3 to 3
- leaf_keys: bfloat16 [64, 64, 56, 128], P('nodes', None, 'heads'), may hold values from -1000 to 1000
- leaf_values: bfloat16 [64, 64, 56, 128], P('nodes', None, 'heads'), may hold values from -3 to 3
- piece_node: int32 [256], replicated, may hold values from 0 to 35, as said below
- mid_parent: int32 [32], replicated, may hold values from 0 to 3
- leaf_parent: int32 [64], replicated, may hold values from 0 to 31
- leaf_len: int32 [64], replicated, may hold values from 1 to 64
- sink_len: int32 [64], replicated, may hold values from 0 to 4
- window_len: int32 [64], replicated, may hold values from 2048 to 4096
Outputs:
- layer_out: bfloat16 [64, 7168], P('heads', 'nodes')
Inputs may be any that keep to these rules, and one draw needn't show every extreme that they name: `piece_node`: every root owns some pieces; a middle node may own none.
All inputs are finite; a program needn't handle non-finite values.
Results may differ from a plain program's by a relative error of at most 0.007.
The roundings to bfloat16 on the way count: a program that leaves them out, or rounds other values in their place, can miss the bound.
Values may be sent and summed in bfloat16 or wider, within the bound.
A program may use at most 64 MiB of HBM per device.

v0:
```python
import math
import jax
import jax.numpy as jnp
from jax import lax
from jax.sharding import PartitionSpec as P

SEG = 128
ROOTS = 4
MIDS = 32
epsilon = 1e-05
negative_fill = -1e30


def joined(part, axis, combine):
    gathered = jax.tree.map(lambda a: lax.all_gather(a, axis), part)

    def take(source):
        return jax.tree.map(lambda a: lax.dynamic_index_in_dim(a, source, 0, False), gathered)

    return lax.fori_loop(
        1, lax.axis_size(axis), lambda source, state: combine(state, take(source)), take(0)
    )


def layer_norm(hidden, norm_gain):
    values = hidden.astype(jnp.float32)
    mean_value = jnp.mean(values, axis=1, keepdims=True)
    centered = values - mean_value
    variance = jnp.mean(centered * centered, axis=1, keepdims=True)
    return (centered * lax.rsqrt(variance + epsilon) * norm_gain[None, :]).astype(jnp.bfloat16)


def lookup(lookup_table, chosen):
    positions = jnp.arange(lookup_table.shape[0], dtype=jnp.int32)
    picked = jnp.where(chosen[:, None] == positions[None, :], lookup_table[None, :], 0)
    return jnp.sum(picked, axis=1)


def tree_rows(piece_node, mid_parent, leaf_parent, leaf_len):
    node_ids = jnp.arange(ROOTS + MIDS, dtype=jnp.int32)
    counts = jnp.sum((piece_node[:, None] == node_ids[None, :]).astype(jnp.int32), axis=0)
    root_node = lookup(mid_parent, leaf_parent)
    mid_node = leaf_parent + ROOTS
    root_len = SEG * lookup(counts, root_node)
    mid_len = SEG * lookup(counts, mid_node)
    finish = root_len + mid_len + leaf_len
    return (root_node, mid_node, root_len, finish)


def piece_rank(piece_node, chosen):
    all_pieces = jnp.arange(piece_node.shape[0], dtype=jnp.int32)
    nodes_here = lookup(piece_node, chosen)
    same = (piece_node[None, :] == nodes_here[:, None]) & (all_pieces[None, :] < chosen[:, None])
    return (nodes_here, jnp.sum(same.astype(jnp.int32), axis=1))


def prefix_allowed(
    node_block, rank_block, root_node, mid_node, root_len, finish, sink_len, window_len
):
    offsets = jnp.arange(SEG, dtype=jnp.int32)
    rel_pos = rank_block[:, None] * SEG + offsets[None, :]
    at_root = node_block[None, :] == root_node[:, None]
    at_mid = node_block[None, :] == mid_node[:, None]
    token_pos = rel_pos[None, :, :] + jnp.where(at_mid, root_len[:, None], 0)[:, :, None]
    inside = (token_pos < sink_len[:, None, None]) | (
        token_pos >= (finish - window_len)[:, None, None]
    )
    return ((at_root | at_mid)[:, :, None] & inside)[:, None, :, :]


def leaf_allowed(finish, leaf_len, sink_len, window_len, leaf_max):
    offsets = jnp.arange(leaf_max, dtype=jnp.int32)
    token_pos = (finish - leaf_len)[:, None] + offsets[None, :]
    inside = (token_pos < sink_len[:, None]) | (token_pos >= (finish - window_len)[:, None])
    return (inside & (offsets[None, :] < leaf_len[:, None]))[:, None, :]


def combine(first_part, second_part):
    highest = jnp.maximum(first_part[0], second_part[0])
    factor_one = jnp.exp(first_part[0] - highest)
    factor_two = jnp.exp(second_part[0] - highest)
    totals = first_part[1] * factor_one + second_part[1] * factor_two
    summed = first_part[2] * factor_one[..., None] + second_part[2] * factor_two[..., None]
    return (highest, totals, summed)


def weigh(scores, allowed, axes):
    masked = jnp.where(allowed, scores, negative_fill)
    maxima = jnp.max(masked, axis=axes)
    expanded = maxima
    for axis_pos in axes:
        expanded = jnp.expand_dims(expanded, axis_pos)
    weights = jnp.where(allowed, jnp.exp(masked - expanded), 0.0).astype(jnp.bfloat16)
    return (maxima, weights)


def on_device(
    hidden,
    norm_gain,
    qkv_weight,
    out_weight,
    prefix_keys,
    prefix_values,
    leaf_keys,
    leaf_values,
    piece_node,
    mid_parent,
    leaf_parent,
    leaf_len,
    sink_len,
    window_len,
):
    node_index = lax.axis_index("nodes")
    req_dev = hidden.shape[0]
    heads_dev = qkv_weight.shape[1]
    head_size = qkv_weight.shape[2] // 3
    seg_dev = prefix_keys.shape[0]
    first_row = node_index * req_dev
    score_scale = 1.0 / math.sqrt(head_size)
    normed = layer_norm(hidden, norm_gain)
    columns = lax.all_to_all(normed, "nodes", split_axis=1, concat_axis=0, tiled=True)
    width_here = columns.shape[1]
    flat_weight = qkv_weight.reshape(width_here, heads_dev * 3 * head_size)
    mixed_rows = lax.psum_scatter(
        jnp.dot(columns, flat_weight, preferred_element_type=jnp.float32),
        "nodes",
        scatter_dimension=0,
        tiled=True,
    )
    mixed_rows = mixed_rows.astype(jnp.bfloat16).reshape(req_dev, heads_dev, 3, head_size)
    query_here = mixed_rows[:, :, 0]
    key_new = mixed_rows[:, :, 1]
    value_new = mixed_rows[:, :, 2]
    query_all = lax.all_gather(query_here, "nodes", axis=0, tiled=True)
    root_node, mid_node, root_len, finish = tree_rows(piece_node, mid_parent, leaf_parent, leaf_len)
    chosen = node_index * seg_dev + jnp.arange(seg_dev, dtype=jnp.int32)
    node_block, rank_block = piece_rank(piece_node, chosen)
    scores = (
        jnp.einsum("rhd,pshd->rhps", query_all, prefix_keys, preferred_element_type=jnp.float32)
        * score_scale
    )
    allowed = prefix_allowed(
        node_block, rank_block, root_node, mid_node, root_len, finish, sink_len, window_len
    )
    maxima, weights = weigh(scores, allowed, (2, 3))
    totals = jnp.sum(weights.astype(jnp.float32), axis=(2, 3))
    summed = jnp.einsum(
        "rhps,pshd->rhd", weights, prefix_values, preferred_element_type=jnp.float32
    )
    merged = joined((maxima, totals, summed), "nodes", combine)
    merged = tuple((lax.dynamic_slice_in_dim(member, first_row, req_dev, 0) for member in merged))
    finish_here = lax.dynamic_slice_in_dim(finish, first_row, req_dev, 0)
    leaf_here = lax.dynamic_slice_in_dim(leaf_len, first_row, req_dev, 0)
    sink_here = lax.dynamic_slice_in_dim(sink_len, first_row, req_dev, 0)
    window_here = lax.dynamic_slice_in_dim(window_len, first_row, req_dev, 0)
    leaf_scores = (
        jnp.einsum("rhd,rjhd->rhj", query_here, leaf_keys, preferred_element_type=jnp.float32)
        * score_scale
    )
    leaf_mask = leaf_allowed(finish_here, leaf_here, sink_here, window_here, leaf_keys.shape[1])
    leaf_max, leaf_weights = weigh(leaf_scores, leaf_mask, (2,))
    leaf_part = (
        leaf_max,
        jnp.sum(leaf_weights.astype(jnp.float32), axis=2),
        jnp.einsum("rhj,rjhd->rhd", leaf_weights, leaf_values, preferred_element_type=jnp.float32),
    )
    own_score = (
        jnp.sum(query_here.astype(jnp.float32) * key_new.astype(jnp.float32), axis=2) * score_scale
    )
    own_part = (
        own_score,
        jnp.ones((req_dev, heads_dev), jnp.float32),
        value_new.astype(jnp.float32),
    )
    merged = combine(combine(merged, leaf_part), own_part)
    attended = (
        (merged[2] / merged[1][..., None])
        .astype(jnp.bfloat16)
        .reshape(req_dev, heads_dev * head_size)
    )
    out_rows = jnp.dot(
        lax.all_gather(attended, "nodes", axis=0, tiled=True),
        out_weight,
        preferred_element_type=jnp.float32,
    )
    return lax.psum_scatter(out_rows, "heads", scatter_dimension=0, tiled=True).astype(jnp.bfloat16)


def solution(mesh):
    return jax.shard_map(
        on_device,
        mesh=mesh,
        in_specs=(
            P("nodes", None),
            P(),
            P("nodes", "heads", None),
            P("heads", "nodes"),
            P("nodes", None, "heads", None),
            P("nodes", None, "heads", None),
            P("nodes", None, "heads", None),
            P("nodes", None, "heads", None),
            P(),
            P(),
            P(),
            P(),
            P(),
            P(),
        ),
        out_specs=P("heads", "nodes"),
        check_vma=False,
    )
```

profile of v0, /device:TPU:2, one launch (start us, length us, event | category | flops | bytes accessed | tf_op | source)
XLA Modules:
  0.0 810.2 jit_solution(8103925422148323476)
XLA Ops:
  6.5 1.5 convert_reduce_fusion.3
  8.7 1.4 multiply_reduce_fusion
  12.4 18.6 %all-to-all-start = ((bf16[1,64,112]{2,0,1:T(2,128)(2,1)}), bf16[1,64,112]{2,0,1:T(2,128)(2,1)S(1)}, u32[]{:S(2)}, u32[]{:S(2)}) async-start(bf16[1,64,112]{2,0,1:T(2,128)(2,1)} %all_to_all.15), calls=%async_computation | async-start | bytes 65536 | tf_op jit(solution)/shard_map/all_to_all | solution.py:121
  36.9 1.1 copy.86
  38.0 1.3 dynamic-slice
  39.3 5.2 all-to-all-done
  44.7 257.9 %all-reduce.3 = bf16[64,2688]{1,0:T(8,128)(2,1)S(1)} all-reduce(f32[64,2688]{1,0:T(8,128)S(1)} %fusion.19), channel_id=6, replica_groups=mesh['nodes'=64,'heads'=8] {'nodes'}, use_global_device_ids=true, to_apply=%region_8.9.clone | all-reduce | flops 172032 | bytes 1032192
  303.3 120.7 %all-gather = bf16[64,7,1,128]{3,1,2,0:T(8,128)(2,1)S(1)} all-gather(bf16[1,7,1,128]{3,1,2,0:T(8,128)(2,1)S(1)} %copy.68), channel_id=2, replica_groups=mesh['nodes'=64,'heads'=8] {'nodes'}, dimensions={0}, use_global_device_ids=true | all-gather | bytes 116480 | tf_op jit(solution)/shard_map/all_gather | solution.py:134
  424.5 2.2 convolution_bitcast_fusion
  426.8 1.2 dynamic_slice.68
  428.0 1.3 dynamic_slice.70
  429.3 1.3 dynamic_slice.69
  433.7 1.3 dynamic-slice.2
  435.7 1.3 compare_and_fusion
  437.0 78.9 %all-gather.4 = f32[64,64,7]{1,2,0:T(8,128)S(1)} all-gather(f32[1,64,7]{1,2,0:T(8,128)S(1)} %bitcast.134), channel_id=3, replica_groups=mesh['nodes'=64,'heads'=8] {'nodes'}, dimensions={0}, use_global_device_ids=true | all-gather | bytes 116480 | tf_op jit(solution)/shard_map/all_gather | solution.py:15
  516.2 82.0 %all-gather.5 = f32[64,64,7]{1,2,0:T(8,128)S(1)} all-gather(f32[1,64,7]{1,2,0:T(8,128)S(1)} %bitcast.136), channel_id=4, replica_groups=mesh['nodes'=64,'heads'=8] {'nodes'}, dimensions={0}, use_global_device_ids=true | all-gather | bytes 116480 | tf_op jit(solution)/shard_map/all_gather | solution.py:15
  598.2 1.1 fusion.16
  599.8 1.0 fusion.14
  602.3 95.5 %while.19 = (s32[]{:T(128)}, f32[64,7]{0,1:T(8,128)S(1)}, f32[64,7]{0,1:T(8,128)S(1)}, f32[64,7,128]{2,1,0:T(8,128)S(1)}, f32[64,64,7]{1,2,0:T(8,128)S(1)}, /*in...) while((s32[]{:T(128)}, f32[64,7]{0,1:T(8,128)S(1)}, ...), condition=%wide.region_12.13_spmd, body=%wide.region_11.12_spmd.sunk | while | flops 174725 | bytes 1172119 | solution.py:20
  602.3 1.0 constant_dynamic-slice_fusion.4
  603.8 1.0 constant_dynamic-slice_fusion.4
  605.3 1.0 constant_dynamic-slice_fusion.4
  606.9 1.0 constant_dynamic-slice_fusion.4
  608.4 1.0 constant_dynamic-slice_fusion.4
  609.9 1.0 constant_dynamic-slice_fusion.4
  611.4 1.0 constant_dynamic-slice_fusion.4
  612.9 1.0 constant_dynamic-slice_fusion.4
  614.4 1.0 constant_dynamic-slice_fusion.4
  615.9 1.0 constant_dynamic-slice_fusion.4
  617.5 1.0 constant_dynamic-slice_fusion.4
  619.0 1.0 constant_dynamic-slice_fusion.4
  620.5 1.0 constant_dynamic-slice_fusion.4
  622.0 1.0 constant_dynamic-slice_fusion.4
  623.5 1.0 constant_dynamic-slice_fusion.4
  625.0 1.0 constant_dynamic-slice_fusion.4
  626.6 1.0 constant_dynamic-slice_fusion.4
  628.1 1.0 constant_dynamic-slice_fusion.4
  629.6 1.0 constant_dynamic-slice_fusion.4
  631.1 1.0 constant_dynamic-slice_fusion.4
  632.6 1.0 constant_dynamic-slice_fusion.4
  634.1 1.0 constant_dynamic-slice_fusion.4
  635.7 1.0 constant_dynamic-slice_fusion.4
  637.2 1.0 constant_dynamic-slice_fusion.4
  638.7 1.0 constant_dynamic-slice_fusion.4
  641.7 1.0 constant_dynamic-slice_fusion.4
  644.7 1.0 constant_dynamic-slice_fusion.4
  647.8 1.0 constant_dynamic-slice_fusion.4
  652.3 1.0 constant_dynamic-slice_fusion.4
  655.4 1.0 constant_dynamic-slice_fusion.4
  658.4 1.0 constant_dynamic-slice_fusion.4
  661.4 1.0 constant_dynamic-slice_fusion.4
  664.5 1.0 constant_dynamic-slice_fusion.4
  667.5 1.0 constant_dynamic-slice_fusion.4
  670.5 1.0 constant_dynamic-slice_fusion.4
  673.5 1.0 constant_dynamic-slice_fusion.4
  676.6 1.0 constant_dynamic-slice_fusion.4
  681.1 1.0 constant_dynamic-slice_fusion.4
  684.2 1.0 constant_dynamic-slice_fusion.4
  687.2 1.0 constant_dynamic-slice_fusion.4
  690.2 1.0 constant_dynamic-slice_fusion.4
  693.3 1.0 constant_dynamic-slice_fusion.4
  696.3 1.0 constant_dynamic-slice_fusion.4
  698.2 80.7 %all-gather.6 = bf16[64,1,896]{2,1,0:T(2,128)(2,1)S(1)} all-gather(bf16[1,1,896]{2,1,0:T(2,128)(2,1)S(1)} %convert_bitcast_fusion), channel_id=1, replica_groups=mesh['nodes'=64,'heads'=8] {'nodes'}, dimensions={0}, use_global_device_ids=true | all-gather | bytes 116480 | tf_op jit(solution)/shard_map/all_gather | solution.py:182
  779.1 23.6 %all-reduce.1 = bf16[64,112]{1,0:T(8,128)(2,1)S(1)} all-reduce(f32[64,112]{1,0:T(8,128)S(1)} %fusion.10), channel_id=7, replica_groups=mesh['nodes'=64,'heads'=8] {'heads'}, use_global_device_ids=true, to_apply=%region_16.17.clone | all-reduce | flops 7168 | bytes 43008
  (318 shorter events, 64.6 us)
Async XLA Ops:
  6.5 417.5 %copy-start = (bf16[4,128,7,128]{3,1,2,0:T(8,128)(2,1)S(1)}, bf16[4,128,7,128]{3,1,2,0:T(8,128)(2,1)}, u32[]{:S(2)}) copy-start(bf16[4,128,7,128]{3,1,2,0:T(8,128)(2,1)} %param.20) | copy-start | bytes 2752516
  6.5 772.4 %copy-start.1 = (bf16[896,112]{0,1:T(8,128)(2,1)S(1)}, bf16[896,112]{0,1:T(8,128)(2,1)}, u32[]{:S(2)}) copy-start(bf16[896,112]{0,1:T(8,128)(2,1)} %param.19) | copy-start | bytes 602116
  12.4 32.1 %all-to-all-start = ((bf16[1,64,112]{2,0,1:T(2,128)(2,1)}), bf16[1,64,112]{2,0,1:T(2,128)(2,1)S(1)}, u32[]{:S(2)}, u32[]{:S(2)}) async-start(bf16[1,64,112]{2,0,1:T(2,128)(2,1)} %all_to_all.15), calls=%async_computation | async-start | bytes 65536 | tf_op jit(solution)/shard_map/all_to_all | solution.py:121
  31.0 570.1 %all-gather.9.cloned.1.call-start = ((), (), s32[]{:S(2)}) async-start(), calls=%async_computation.1 | async-start | bytes 14909440 | tf_op jit(solution)/shard_map/all_gather | solution.py:15
Sparse Core Ops, SparseCore 0:
  426.9 174.2 all-gather.8
where the time goes:
time: 813 us; the launch traced here: 810 us
  blocking collectives  644 us (79%)
  local copies, waits for them, and re-layouts  84.4 us (10%)
  other arithmetic  32.2 us (4%)
  starting transfers between devices  18.7 us (2%)
  between operations  18 us (2%)
    unnamed x2, blocking collectives  281 us
    all_gather x2, blocking collectives, joined(): gathered = jax.tree.map(lambda a: lax.all_gather(a, axis), part)  161 us
    all_gather x1, blocking collectives, on_device(): query_all = lax.all_gather(query_here, 'nodes', axis=0, tiled=True)  121 us
    all_gather x1, blocking collectives, on_device(): lax.all_gather(attended, 'nodes', axis=0, tiled=True)  80.7 us
    dynamic_slice x66, local copies, waits for them, and re-layouts, take(): lax.dynamic_index_in_dim(a, source, 0, False)  61.8 us
    add x63, other arithmetic, combine(): first_part[2] * factor_one[..., None]  19.3 us
    all_to_all x1, starting transfers between devices, on_device(): lax.all_to_all(normed, 'nodes', split_axis=1, concat_axis=0, tiled=True)  18.6 us
  transfers between devices with their start and end apart: 2, of which 2 were waited for; matrix products, arithmetic and copies ran while one was open for 2% of the time, Pallas kernels for 0%

commit v1 on v0

--- a/solution.py
+++ b/solution.py
@@ -118,7 +118,10 @@
     first_row = node_index * req_dev
     score_scale = 1.0 / math.sqrt(head_size)
     normed = layer_norm(hidden, norm_gain)
-    columns = lax.all_to_all(normed, "nodes", split_axis=1, concat_axis=0, tiled=True)
+    columns = jnp.concatenate(
+        lax.all_to_all(jnp.stack(jnp.split(normed, lax.axis_size("nodes"), axis=1)), "nodes", 0, 0),
+        axis=0,
+    )
     width_here = columns.shape[1]
     flat_weight = qkv_weight.reshape(width_here, heads_dev * 3 * head_size)
     mixed_rows = lax.psum_scatter(

time: 813 us -> 851 us (1.047)
  local copies, waits for them, and re-layouts: 84.4 us -> 123 us
    unnamed x6 -> x69, local copies, waits for them, and re-layouts: 2.6 us -> 40.7 us
where the time goes in v1:
time: 851 us; the launch traced here: 848 us
  blocking collectives  644 us (76%)
  local copies, waits for them, and re-layouts  123 us (14%)
  other arithmetic  32.3 us (4%)
  starting transfers between devices  18.7 us (2%)
  between operations  18 us (2%)
    unnamed x2, blocking collectives  281 us
    all_gather x2, blocking collectives, joined(): gathered = jax.tree.map(lambda a: lax.all_gather(a, axis), part)  161 us
    all_gather x1, blocking collectives, on_device(): query_all = lax.all_gather(query_here, 'nodes', axis=0, tiled=True)  121 us
    all_gather x1, blocking collectives, on_device(): lax.all_gather(attended, 'nodes', axis=0, tiled=True)  80.7 us
    dynamic_slice x66, local copies, waits for them, and re-layouts, take(): lax.dynamic_index_in_dim(a, source, 0, False)  61.8 us
    unnamed x69, local copies, waits for them, and re-layouts  40.7 us
    add x63, other arithmetic, combine(): first_part[2] * factor_one[..., None]  19.3 us
    all_to_all x1, starting transfers between devices, on_device(): lax.all_to_all(jnp.stack(jnp.split(normed, lax.axis_size('nodes'), axis=1...  18.6 us
  transfers between devices with their start and end apart: 2, of which 2 were waited for; matrix products, arithmetic and copies ran while one was open for 2% of the time, Pallas kernels for 0%

profile of v1, /device:TPU:2, one launch (start us, length us, event | category | flops | bytes accessed | tf_op | source)
XLA Modules:
  0.0 848.4 jit_solution(3173547713119589487)
XLA Ops:
  6.5 1.5 convert_reduce_fusion.2
  8.7 1.4 multiply_reduce_fusion
  50.5 18.6 %all-to-all-start = ((bf16[64,1,112]{2,1,0:T(2,128)(2,1)}), bf16[64,1,112]{2,1,0:T(2,128)(2,1)S(1)}, u32[]{:S(2)}, u32[]{:S(2)}) async-start(bf16[64,1,112]{2,1,0:T(2,128)(2,1)} %constant_dynamic-update-slice_fusion), calls=%async_computation | async-start | bytes 65536 | tf_op jit(solution)/shard_map/all_to_all | solution.py:122
  74.9 1.1 copy.72
  76.1 1.3 dynamic-slice
  77.3 5.2 all-to-all-done
  82.8 257.9 %all-reduce.3 = bf16[64,2688]{1,0:T(8,128)(2,1)S(1)} all-reduce(f32[64,2688]{1,0:T(8,128)S(1)} %fusion.19), channel_id=6, replica_groups=mesh['nodes'=64,'heads'=8] {'nodes'}, use_global_device_ids=true, to_apply=%region_8.9.clone | all-reduce | flops 172032 | bytes 1032192
  341.4 120.7 %all-gather = bf16[64,7,1,128]{3,1,2,0:T(8,128)(2,1)S(1)} all-gather(bf16[1,7,1,128]{3,1,2,0:T(8,128)(2,1)S(1)} %copy.54), channel_id=2, replica_groups=mesh['nodes'=64,'heads'=8] {'nodes'}, dimensions={0}, use_global_device_ids=true | all-gather | bytes 116480 | tf_op jit(solution)/shard_map/all_gather | solution.py:137
  462.6 2.2 convolution_bitcast_fusion
  464.9 1.2 dynamic_slice.68
  466.1 1.3 dynamic_slice.70
  467.4 1.3 dynamic_slice.69
  471.8 1.3 dynamic-slice.2
  473.7 1.3 compare_and_fusion
  475.1 78.9 %all-gather.4 = f32[64,64,7]{1,2,0:T(8,128)S(1)} all-gather(f32[1,64,7]{1,2,0:T(8,128)S(1)} %bitcast.390), channel_id=3, replica_groups=mesh['nodes'=64,'heads'=8] {'nodes'}, dimensions={0}, use_global_device_ids=true | all-gather | bytes 116480 | tf_op jit(solution)/shard_map/all_gather | solution.py:15
  554.3 82.0 %all-gather.5 = f32[64,64,7]{1,2,0:T(8,128)S(1)} all-gather(f32[1,64,7]{1,2,0:T(8,128)S(1)} %bitcast.392), channel_id=4, replica_groups=mesh['nodes'=64,'heads'=8] {'nodes'}, dimensions={0}, use_global_device_ids=true | all-gather | bytes 116480 | tf_op jit(solution)/shard_map/all_gather | solution.py:15
  636.3 1.1 fusion.16
  637.9 1.0 fusion.14
  640.3 95.6 %while.19 = (s32[]{:T(128)}, f32[64,7]{0,1:T(8,128)S(1)}, f32[64,7]{0,1:T(8,128)S(1)}, f32[64,7,128]{2,1,0:T(8,128)S(1)}, f32[64,64,7]{1,2,0:T(8,128)S(1)}, /*in...) while((s32[]{:T(128)}, f32[64,7]{0,1:T(8,128)S(1)}, ...), condition=%wide.region_12.13_spmd, body=%wide.region_11.12_spmd.sunk | while | flops 174725 | bytes 1172119 | solution.py:20
  640.4 1.0 constant_dynamic-slice_fusion.4
  641.9 1.0 constant_dynamic-slice_fusion.4
  643.4 1.0 constant_dynamic-slice_fusion.4
  644.9 1.0 constant_dynamic-slice_fusion.4
  646.5 1.0 constant_dynamic-slice_fusion.4
  648.0 1.0 constant_dynamic-slice_fusion.4
  649.5 1.0 constant_dynamic-slice_fusion.4
  651.0 1.0 constant_dynamic-slice_fusion.4
  652.5 1.0 constant_dynamic-slice_fusion.4
  654.1 1.0 constant_dynamic-slice_fusion.4
  655.6 1.0 constant_dynamic-slice_fusion.4
  657.1 1.0 constant_dynamic-slice_fusion.4
  658.6 1.0 constant_dynamic-slice_fusion.4
  660.1 1.0 constant_dynamic-slice_fusion.4
  661.6 1.0 constant_dynamic-slice_fusion.4
  663.2 1.0 constant_dynamic-slice_fusion.4
  664.7 1.0 constant_dynamic-slice_fusion.4
  666.2 1.0 constant_dynamic-slice_fusion.4
  667.7 1.0 constant_dynamic-slice_fusion.4
  669.2 1.0 constant_dynamic-slice_fusion.4
  670.7 1.0 constant_dynamic-slice_fusion.4
  672.3 1.0 constant_dynamic-slice_fusion.4
  673.8 1.0 constant_dynamic-slice_fusion.4
  675.3 1.0 constant_dynamic-slice_fusion.4
  676.8 1.0 constant_dynamic-slice_fusion.4
  679.9 1.0 constant_dynamic-slice_fusion.4
  684.4 1.0 constant_dynamic-slice_fusion.4
  685.9 1.0 constant_dynamic-slice_fusion.4
  690.5 1.0 constant_dynamic-slice_fusion.4
  692.0 1.0 constant_dynamic-slice_fusion.4
  696.6 1.0 constant_dynamic-slice_fusion.4
  698.1 1.0 constant_dynamic-slice_fusion.4
  702.6 1.0 constant_dynamic-slice_fusion.4
  704.1 1.0 constant_dynamic-slice_fusion.4
  708.7 1.0 constant_dynamic-slice_fusion.4
  713.2 1.0 constant_dynamic-slice_fusion.4
  714.8 1.0 constant_dynamic-slice_fusion.4
  719.3 1.0 constant_dynamic-slice_fusion.4
  720.8 1.0 constant_dynamic-slice_fusion.4
  725.4 1.0 constant_dynamic-slice_fusion.4
  726.9 1.0 constant_dynamic-slice_fusion.4
  731.5 1.0 constant_dynamic-slice_fusion.4
  733.0 1.0 constant_dynamic-slice_fusion.4
  736.4 80.7 %all-gather.6 = bf16[64,1,896]{2,1,0:T(2,128)(2,1)S(1)} all-gather(bf16[1,1,896]{2,1,0:T(2,128)(2,1)S(1)} %convert_bitcast_fusion), channel_id=1, replica_groups=mesh['nodes'=64,'heads'=8] {'nodes'}, dimensions={0}, use_global_device_ids=true | all-gather | bytes 116480 | tf_op jit(solution)/shard_map/all_gather | solution.py:185
  817.3 23.6 %all-reduce.1 = bf16[64,112]{1,0:T(8,128)(2,1)S(1)} all-reduce(f32[64,112]{1,0:T(8,128)S(1)} %fusion.10), channel_id=7, replica_groups=mesh['nodes'=64,'heads'=8] {'heads'}, use_global_device_ids=true, to_apply=%region_16.17.clone | all-reduce | flops 7168 | bytes 43008
  (381 shorter events, 102.8 us)
Async XLA Ops:
  6.5 455.5 %copy-start = (bf16[4,128,7,128]{3,1,2,0:T(8,128)(2,1)S(1)}, bf16[4,128,7,128]{3,1,2,0:T(8,128)(2,1)}, u32[]{:S(2)}) copy-start(bf16[4,128,7,128]{3,1,2,0:T(8,128)(2,1)} %param.20) | copy-start | bytes 2752516
  6.5 810.6 %copy-start.1 = (bf16[896,112]{0,1:T(8,128)(2,1)S(1)}, bf16[896,112]{0,1:T(8,128)(2,1)}, u32[]{:S(2)}) copy-start(bf16[896,112]{0,1:T(8,128)(2,1)} %param.19) | copy-start | bytes 602116
  50.5 32.1 %all-to-all-start = ((bf16[64,1,112]{2,1,0:T(2,128)(2,1)}), bf16[64,1,112]{2,1,0:T(2,128)(2,1)S(1)}, u32[]{:S(2)}, u32[]{:S(2)}) async-start(bf16[64,1,112]{2,1,0:T(2,128)(2,1)} %constant_dynamic-update-slice_fusion), calls=%async_computation | async-start | bytes 65536 | tf_op jit(solution)/shard_map/all_to_all | solution.py:122
  69.1 570.1 %all-gather.9.cloned.1.call-start = ((), (), s32[]{:S(2)}) async-start(), calls=%async_computation.1 | async-start | bytes 14909440 | tf_op jit(solution)/shard_map/all_gather | solution.py:15
Sparse Core Ops, SparseCore 0:
  465.0 174.2 all-gather.8
